TPU v7x, 128 devices: a whole 4x4x4 slice. The times are simulated.
128 devices in a mesh: row: 4 (over y_lo, core), col: 32 (over y_hi, x, z).
Axes of the slice: x: 4, y: 4 (y_hi: 2, y_lo: 2; y = y_hi * 2 + y_lo), z: 4, core: 2. Of those that a mesh axis runs over, the one named last changes fastest.
Arguments:
- row_coords: bfloat16 [3, 4096, 512], P(None, ('row', 'col')), may hold values from -10 to 10, as said below
- col_coords: bfloat16 [3, 32768, 512], P(None, 'col'), may hold values from -10 to 10, as said below
- start_block: float32 [32768, 64], P('col'), may hold values from -0.03125 to 0.03125
Outputs:
- basis: float32 [4096, 64], P('row')
- image: float32 [32768, 64], P('col')
Inputs may be any that keep to these rules, and one draw needn't show every extreme that they name: `row_coords`: coordinates of frames of one molecule in varying conformations. `col_coords`: coordinates of frames of the same molecule in varying conformations.
All inputs are finite; a program needn't handle non-finite values.
Results may differ from a plain program's by a relative error of at most 0.0073.
Values may be sent and summed in bfloat16 or wider, within the bound.
No kernel may reach another device: no remote copies, remote signals or barrier semaphores. Data moves between devices by JAX's collectives and lax.ppermute only.
A program may use at most 128 MiB of HBM per device.

v0:
```python
import math
import jax
import jax.numpy as jnp
from jax import lax
from jax.sharding import PartitionSpec as P

ATOMS = 512
NEWTON = 8


def from_everyone(shard, axis):
    copies = jnp.broadcast_to(shard, (lax.axis_size(axis), *shard.shape))
    return lax.all_to_all(copies, axis, split_axis=0, concat_axis=0, tiled=True)


def over_copies(shard, axis):
    everything = from_everyone(shard, axis)
    return jnp.sum(everything, axis=0)


def filled_up(lines, devices):
    spare = -len(lines) % devices
    return jnp.pad(lines, [(0, spare)] + [(0, 0)] * (lines.ndim - 1))


def joined_along(pieces, dim):
    dims = list(pieces.shape[1:])
    dims[dim] *= pieces.shape[0]
    return jnp.moveaxis(pieces, 0, dim).reshape(dims)


def collect(shard, axis, dim):
    return joined_along(from_everyone(shard, axis), dim)


def cut_along(shard, dim, devices):
    dims = shard.shape
    pieces = shard.reshape(*dims[:dim], devices, dims[dim] // devices, *dims[dim + 1 :])
    return jnp.moveaxis(pieces, dim, 0)


def sum_at_owner(shard, axis, dim):
    pieces = cut_along(shard, dim, lax.axis_size(axis))
    arrived = lax.all_to_all(pieces, axis, split_axis=0, concat_axis=0, tiled=True)
    return arrived.sum(axis=0)


def total_of(shard, axes):
    padded = filled_up(shard, lax.axis_size(axes))
    whole = collect(sum_at_owner(padded, axes, 0), axes, 0)
    return lax.slice_in_dim(whole, 0, len(shard)).reshape(shard.shape)


def in_one(arrays, axis):
    ends = [0]
    for a in arrays:
        ends.append(ends[-1] + a.size)
    subtotal = total_of(jnp.concatenate([a.ravel() for a in arrays]), axis)
    return tuple((subtotal[b:e].reshape(a.shape) for a, b, e in zip(arrays, ends, ends[1:])))


def packed_total(arrays, axis):
    ends = [0]
    for a in arrays:
        ends.append(ends[-1] + a.size)
    subtotal = over_copies(jnp.concatenate([a.ravel() for a in arrays]), axis)
    return tuple((subtotal[b:e].reshape(a.shape) for a, b, e in zip(arrays, ends, ends[1:])))


def centre_frames(coords):
    shifted = coords.astype(jnp.float32)
    shifted = shifted - jnp.mean(shifted, axis=2, keepdims=True)
    rounded = shifted.astype(jnp.bfloat16)
    widened = lax.optimization_barrier(rounded).astype(jnp.float32)
    return (rounded, jnp.sum(widened * widened, axis=(0, 2)) / ATOMS)


def two_minor(matrix, upper, lower, left, right):
    return matrix[upper][left] * matrix[lower][right] - matrix[lower][left] * matrix[upper][right]


def squared_rmsd(cross, row_norm, col_norm):
    part = [[cross[first, second] for second in range(3)] for first in range(3)]
    trace = part[0][0] + part[1][1] + part[2][2]
    matrix = [[None] * 4 for index in range(4)]
    matrix[0][0] = trace
    matrix[1][1] = 2.0 * part[0][0] - trace
    matrix[2][2] = 2.0 * part[1][1] - trace
    matrix[3][3] = 2.0 * part[2][2] - trace
    matrix[0][1] = part[1][2] - part[2][1]
    matrix[0][2] = part[2][0] - part[0][2]
    matrix[0][3] = part[0][1] - part[1][0]
    matrix[1][2] = part[0][1] + part[1][0]
    matrix[1][3] = part[2][0] + part[0][2]
    matrix[2][3] = part[1][2] + part[2][1]
    for first in range(4):
        for second in range(first):
            matrix[first][second] = matrix[second][first]
    key_determinant = (
        two_minor(matrix, 0, 1, 0, 1) * two_minor(matrix, 2, 3, 2, 3)
        - two_minor(matrix, 0, 1, 0, 2) * two_minor(matrix, 2, 3, 1, 3)
        + two_minor(matrix, 0, 1, 0, 3) * two_minor(matrix, 2, 3, 1, 2)
        + two_minor(matrix, 0, 1, 1, 2) * two_minor(matrix, 2, 3, 0, 3)
        - two_minor(matrix, 0, 1, 1, 3) * two_minor(matrix, 2, 3, 0, 2)
        + two_minor(matrix, 0, 1, 2, 3) * two_minor(matrix, 2, 3, 0, 1)
    )
    cross_determinant = (
        part[0][0] * (part[1][1] * part[2][2] - part[1][2] * part[2][1])
        - part[0][1] * (part[1][0] * part[2][2] - part[1][2] * part[2][0])
        + part[0][2] * (part[1][0] * part[2][1] - part[1][1] * part[2][0])
    )
    squares = sum(
        (part[first][second] * part[first][second] for first in range(3) for second in range(3))
    )
    coeff_two = -2.0 * squares
    coeff_one = -8.0 * cross_determinant
    root_guess = 0.5 * (row_norm + col_norm)
    for sweep in range(NEWTON):
        poly_value = (
            (root_guess * root_guess + coeff_two) * root_guess + coeff_one
        ) * root_guess + key_determinant
        poly_slope = (4.0 * root_guess * root_guess + 2.0 * coeff_two) * root_guess + coeff_one
        root_guess = root_guess - poly_value / poly_slope
    return row_norm + col_norm - 2.0 * root_guess


def body(row_coords, col_coords, start_block):
    highest = lax.Precision.HIGHEST
    cols, col_norm = centre_frames(col_coords)
    rows, row_norm = centre_frames(lax.all_gather(row_coords, "col", axis=1, tiled=True))
    cross = jnp.einsum("ark,bck->abrc", rows, cols, preferred_element_type=jnp.float32) / ATOMS
    dist = squared_rmsd(cross, row_norm[:, None], col_norm[None, :])
    row_count, col_count = dist.shape
    total_rows = row_count * lax.axis_size("row")
    total_cols = col_count * lax.axis_size("col")
    block_mean = over_copies(jnp.sum(start_block, axis=0), "col") / total_cols
    panel_terms = (
        jnp.dot(dist, start_block - block_mean[None, :], precision=highest),
        jnp.sum(dist, axis=1),
    )
    summed = in_one((panel_terms[0], panel_terms[1]), "col")
    product = summed[0]
    stats = jax.tree.map(
        lambda part: over_copies(part, "row"),
        (jnp.dot(product.T, product, precision=highest), jnp.sum(product, axis=0)),
    )
    mean_row = stats[1] / total_rows
    panel = -0.5 * (summed[0] - mean_row[None, :])
    gram = 0.25 * (stats[0] / total_rows - jnp.outer(mean_row, mean_row))
    lower = jnp.linalg.cholesky(gram)
    basis = lax.linalg.triangular_solve(lower, panel, left_side=False, lower=True, transpose_a=True)
    row_totals = summed[1]
    column_terms = (
        jnp.dot(dist.T, basis, precision=highest),
        jnp.dot(row_totals, basis, precision=highest),
    )
    reduced = packed_total((column_terms[0], column_terms[1]), "row")
    image = -0.5 * (reduced[0] - reduced[1][None, :] / total_cols) / math.sqrt(total_rows)
    return (basis, image)


def solution(mesh):
    in_specs = (P(None, ("row", "col"), None), P(None, "col", None), P("col", None))
    out_specs = (P("row", None), P("col", None))
    return jax.shard_map(body, mesh=mesh, in_specs=in_specs, out_specs=out_specs, check_vma=False)
```

profile of v0, /device:TPU:1, one launch (start us, length us, event | category | flops | bytes accessed | tf_op | source)
XLA Modules:
  0.0 247.1 jit_solution(10567978950915025042)
XLA Ops:
  7.9 1.3 reduce_sum.112
  9.8 11.3 %all-to-all-start = ((f32[32,1,64]{2,1,0:T(1,128)}), f32[32,1,64]{2,1,0:T(1,128)S(1)}, u32[]{:S(2)}, u32[]{:S(2)}) async-start(f32[32,1,64]{2,1,0:T(1,128)} %broadcast_in_dim.11), calls=%async_computation | async-start | bytes 32768 | tf_op jit(solution)/shard_map/all_to_all | solution.py:13
  21.1 2.4 convert_reduce_fusion
  24.4 1.7 copy-done.3
  26.8 3.0 %all-to-all-done = f32[32,1,64]{2,1,0:T(1,128)S(1)} async-done(((f32[32,1,64]{2,1,0:T(1,128)}), f32[32,1,64]{2,1,0:T(1,128)S(1)}, u32[]{:S(2)}, u32[]{:S(2)}) %all-to-all-start) | async-done | bytes 8224 | tf_op jit(solution)/shard_map/all_to_all | solution.py:13
  29.8 57.4 %all-gather.2.cloned.1.call-done = bf16[3,1024,512]{2,1,0:T(8,128)(2,1)} async-done(((bf16[3,32,512]{2,1,0:T(8,128)(2,1)}), bf16[3,1024,512]{2,1,0:T(8,128)(2,1)}) %all-gather.2.cloned.1.call-update) | async-done | bytes 3145744 | tf_op jit(solution)/shard_map/all_gather | solution.py:130
  87.2 2.5 %convert_reduce_fusion.1 = f32[3,1024]{1,0:T(4,128)S(1)} fusion(bf16[3,1024,512]{2,1,0:T(8,128)(2,1)} %all-gather.2.cloned.1.call-done), kind=kLoop, calls=%fused_computation.13 | loop fusion | flops 3142656 | bytes 3158016 | tf_op jit(solution)/shard_map/reduce_sum | solution.py:72
  91.0 16.0 %multiply_bitcast_fusion = f32[3,3,1024,1024]{2,3,0,1:T(8,128)} fusion(bf16[3,1024,512]{2,1,0:T(8,128)(2,1)S(1)} %copy-done.4, bf16[3,1024,512]{2,1,0:T(8,128)(2,1)S(1)} %fusion.6), kind=kOutput, calls=%fused_computation | convolution fusion | flops 9673113600 | bytes 44040192 | tf_op jit(solution)/shard_map/ark,bck->abrc/dot_general | solution.py:131
  107.7 35.8 %fusion.69 = (f32[1024]{0:T(1024)S(1)}, f32[1024,1024]{0,1:T(8,128)S(1)}) fusion(f32[3,3,1024,1024]{2,3,0,1:T(8,128)} %multiply_bitcast_fusion, f32[1024]{0:T(1024)S(1)} %broadcast_multiply_fusion.2, f32[1024]{0:T(1024)S(1)} %broadcast_multiply_fusion.3), kind=kLoop, calls=%fused_computation.119 | loop fusion | flops 210762752 | bytes 41955328 | tf_op jit(solution)/shard_map/reduce_sum | solution.py:139
  143.5 1.9 copy-done
  145.4 6.8 %fusion.61 = f32[1024,64]{1,0:T(8,128)S(1)} fusion(f32[1024,1024]{0,1:T(8,128)S(1)} %get-tuple-element.11, f32[1024,64]{0,1:T(8,128)S(1)} %copy-done.6, f32[64]{0:T(128)S(1)} %broadcast_multiply_fusion.5), kind=kOutput, calls=%fused_computation.96 | convolution fusion | flops 805371904 | bytes 4718848 | tf_op jit(solution)/shard_map/dot_general | solution.py:138
  152.7 14.3 %all_to_all.38 = f32[32,1,2080]{2,1,0:T(1,128)S(1)} all-to-all(f32[32,1,2080]{2,1,0:T(1,128)S(1)} %all_to_all.26), channel_id=1, replica_groups=mesh['row'=4,'col'=32] {'col'}, dimensions={0} | all-to-all | bytes 532480 | tf_op jit(solution)/shard_map/all_to_all | solution.py:44
  167.4 12.9 %all_to_all.39 = f32[32,1,2080]{2,1,0:T(1,128)S(1)} all-to-all(f32[32,1,2080]{2,1,0:T(1,128)S(1)} %broadcast_in_dim.12), channel_id=1, replica_groups=mesh['row'=4,'col'=32] {'col'}, dimensions={0} | all-to-all | bytes 532480 | tf_op jit(solution)/shard_map/all_to_all | solution.py:13
  182.0 7.8 %all-to-all-start.3 = ((f32[4,1,64]{2,1,0:T(1,128)}), f32[4,1,64]{2,1,0:T(1,128)S(1)}, u32[]{:S(2)}, u32[]{:S(2)}) async-start(f32[4,1,64]{2,1,0:T(1,128)} %broadcast_in_dim.14), calls=%async_computation.3 | async-start | bytes 4096 | tf_op jit(solution)/shard_map/all_to_all | solution.py:13
  189.7 1.0 fusion.56
  191.8 1.0 all-to-all-done.3
  192.8 3.9 %all-to-all-start.4 = ((f32[4,1,4096]{2,1,0:T(1,128)}), f32[4,1,4096]{2,1,0:T(1,128)S(1)}, u32[]{:S(2)}, u32[]{:S(2)}) async-start(f32[4,1,4096]{2,1,0:T(1,128)} %reshape.92), calls=%async_computation.4 | async-start | bytes 131072 | tf_op jit(solution)/shard_map/all_to_all | solution.py:13
  196.7 3.2 %all-to-all-done.4 = f32[4,1,4096]{2,1,0:T(1,128)S(1)} async-done(((f32[4,1,4096]{2,1,0:T(1,128)}), f32[4,1,4096]{2,1,0:T(1,128)S(1)}, u32[]{:S(2)}, u32[]{:S(2)}) %all-to-all-start.4) | async-done | bytes 65568 | tf_op jit(solution)/shard_map/all_to_all | solution.py:13
  201.6 5.8 %cholesky.16 = f32[64,64]{1,0:T(8,128)S(1)} custom-call(f32[64,64]{1,0:T(8,128)S(1)} %fusion.66), custom_call_target="Cholesky" | custom-call | tf_op jit(solution)/shard_map/jit(cholesky)/cholesky | solution.py:150
  208.8 4.9 %custom-call.6 = f32[1,64,64]{1,2,0:T(8,128)S(1)} custom-call(f32[1,64,64]{2,1,0:T(8,128)S(1)} %fusion.64), custom_call_target="InvertDiagBlocksLowerTriangular" | custom-call | tf_op jit(solution)/shard_map/triangular_solve | solution.py:151
  214.5 5.3 %fusion.70 = f32[1024,64]{1,0:T(8,128)S(1)} fusion(f32[1024,1024]{0,1:T(8,128)} %copy-done, f32[1024,64]{0,1:T(8,128)S(1)} %fusion.53), kind=kOutput, calls=%fused_computation.120 | convolution fusion | flops 805306368 | bytes 4718592 | tf_op jit(solution)/shard_map/dot_general | solution.py:154
  220.8 17.3 %all_to_all.40 = f32[4,1,65600]{2,1,0:T(1,128)S(1)} all-to-all(f32[4,1,65600]{2,1,0:T(1,128)S(1)} %broadcast_in_dim.30), channel_id=1, replica_groups=mesh['row'=4,'col'=32] {'row'}, dimensions={0} | all-to-all | bytes 2099200 | tf_op jit(solution)/shard_map/all_to_all | solution.py:13
  238.1 1.0 reduce_sum.119
  239.4 0.9 copy.65
  (59 shorter events, 13.3 us)
Async XLA Ops:
  7.2 16.4 %copy-start.1 = (bf16[3,1024,512]{2,1,0:T(8,128)(2,1)S(1)}, bf16[3,1024,512]{2,1,0:T(8,128)(2,1)}, u32[]{:S(2)}) copy-start(bf16[3,1024,512]{2,1,0:T(8,128)(2,1)} %param.4) | copy-start | bytes 9437188
  7.2 80.0 %all-gather.2.cloned.1.call-start = ((), (), s32[]{:S(2)}) async-start(), calls=%async_computation.6 | async-start | bytes 3244032 | tf_op jit(solution)/shard_map/all_gather | solution.py:130
  9.8 19.9 %all-to-all-start = ((f32[32,1,64]{2,1,0:T(1,128)}), f32[32,1,64]{2,1,0:T(1,128)S(1)}, u32[]{:S(2)}, u32[]{:S(2)}) async-start(f32[32,1,64]{2,1,0:T(1,128)} %broadcast_in_dim.11), calls=%async_computation | async-start | bytes 32768 | tf_op jit(solution)/shard_map/all_to_all | solution.py:13
  24.4 1.7 copy-start.3
  87.2 2.8 %copy-start.2 = (bf16[3,1024,512]{2,1,0:T(8,128)(2,1)S(1)}, bf16[3,1024,512]{2,1,0:T(8,128)(2,1)}, u32[]{:S(2)}) copy-start(bf16[3,1024,512]{2,1,0:T(8,128)(2,1)} %all-gather.2.cloned.1.call-done) | copy-start | bytes 9437188
  87.2 3.8 %copy-start.4 = (bf16[3,1024,512]{2,1,0:T(8,128)(2,1)S(1)}, bf16[3,1024,512]{2,1,0:T(8,128)(2,1)}, u32[]{:S(2)}) copy-start(bf16[3,1024,512]{2,1,0:T(8,128)(2,1)} %copy-done.3) | copy-start | bytes 9437188
  107.7 37.7 %copy-start.6 = (f32[1024,64]{0,1:T(8,128)S(1)}, f32[1024,64]{0,1:T(8,128)}, u32[]{:S(2)}) copy-start(f32[1024,64]{0,1:T(8,128)} %param.5) | copy-start | bytes 786436
  143.5 1.9 copy-start
  182.0 10.8 %all-to-all-start.3 = ((f32[4,1,64]{2,1,0:T(1,128)}), f32[4,1,64]{2,1,0:T(1,128)S(1)}, u32[]{:S(2)}, u32[]{:S(2)}) async-start(f32[4,1,64]{2,1,0:T(1,128)} %broadcast_in_dim.14), calls=%async_computation.3 | async-start | bytes 4096 | tf_op jit(solution)/shard_map/all_to_all | solution.py:13
  192.8 7.2 %all-to-all-start.4 = ((f32[4,1,4096]{2,1,0:T(1,128)}), f32[4,1,4096]{2,1,0:T(1,128)S(1)}, u32[]{:S(2)}, u32[]{:S(2)}) async-start(f32[4,1,4096]{2,1,0:T(1,128)} %reshape.92), calls=%async_computation.4 | async-start | bytes 131072 | tf_op jit(solution)/shard_map/all_to_all | solution.py:13
  214.5 23.7 %copy-start.5 = (f32[1024,64]{0,1:T(8,128)}, f32[1024,64]{0,1:T(8,128)S(1)}, u32[]{:S(2)}) copy-start(f32[1024,64]{0,1:T(8,128)S(1)} %fusion.53) | copy-start | bytes 786436
Sparse Core Ops, SparseCore 0:
  11.1 76.0 all-gather.1
where the time goes:
time: 248 us; the launch traced here: 247 us
  waiting for transfers between devices  65.3 us (26%)
  other arithmetic  60.1 us (24%)
  blocking collectives  44.6 us (18%)
  matrix products  30.1 us (12%)
  starting transfers between devices  23.1 us (9%)
  between operations  14.3 us (6%)
  local copies, waits for them, and re-layouts  9.61 us (4%)
    all_gather x1, waiting for transfers between devices, body(): lax.all_gather(row_coords, 'col', axis=1, tiled=True)  57.4 us
    reduce_sum x1, other arithmetic, body(): jnp.sum(dist, axis=1)  35.8 us
    all_to_all x2, blocking collectives, from_everyone(): return lax.all_to_all(copies, axis, split_axis=0, concat_axis=0, tiled=True)  30.3 us
    all_to_all x3, starting transfers between devices, from_everyone(): return lax.all_to_all(copies, axis, split_axis=0, concat_axis=0, tiled=True)  23 us
    dot_general x1, matrix products, body(): jnp.einsum('ark,bck->abrc', rows, cols, preferred_element_type=jnp.float32)  16 us
    all_to_all x1, blocking collectives, sum_at_owner(): lax.all_to_all(pieces, axis, split_axis=0, concat_axis=0, tiled=True)  14.3 us
    all_to_all x3, waiting for transfers between devices, from_everyone(): return lax.all_to_all(copies, axis, split_axis=0, concat_axis=0, tiled=True)  7.21 us
    dot_general x1, matrix products, body(): jnp.dot(dist, start_block - block_mean[None, :], precision=highest)  6.79 us
  transfers between devices with their start and end apart: 4, of which 4 were waited for; matrix products, arithmetic and copies ran while one was open for 3% of the time, Pallas kernels for 0%

commit v1 on v0

--- a/solution.py
+++ b/solution.py
@@ -6,6 +6,13 @@
 
 ATOMS = 512
 NEWTON = 8
+
+
+def map_samples_all(arr, dim_no):
+    return jnp.concatenate(
+        jax.lax.all_to_all(jnp.stack([arr] * jax.lax.psum(1, axis_name="col"), 0), "col", 0, 0),
+        dim_no,
+    )
 
 
 def from_everyone(shard, axis):
@@ -127,7 +134,7 @@
 def body(row_coords, col_coords, start_block):
     highest = lax.Precision.HIGHEST
     cols, col_norm = centre_frames(col_coords)
-    rows, row_norm = centre_frames(lax.all_gather(row_coords, "col", axis=1, tiled=True))
+    rows, row_norm = centre_frames(map_samples_all(row_coords, 1))
     cross = jnp.einsum("ark,bck->abrc", rows, cols, preferred_element_type=jnp.float32) / ATOMS
     dist = squared_rmsd(cross, row_norm[:, None], col_norm[None, :])
     row_count, col_count = dist.shape

time: 248 us -> 227 us (0.915)
  waiting for transfers between devices: 65.3 us -> 37.7 us
  blocking collectives: 44.6 us -> 70.2 us
  between operations: 14.3 us -> 0.94 us
  starting transfers between devices: 23.1 us -> 15.8 us
  local copies, waits for them, and re-layouts: 9.61 us -> 12.8 us
    all_gather x1 -> x0, waiting for transfers between devices: 57.4 us -> none  [body(): lax.all_gather(row_coords, 'col', axis=1, tiled=True)]
    all_to_all x0 -> x1, waiting for transfers between devices: none -> 33.5 us  [map_samples_all(): jax.lax.all_to_all(jnp.stack([arr] * jax.lax.psum(1, axis_name='col'), 0)...]
    all_to_all x2 -> x3, blocking collectives: 30.3 us -> 50.1 us  [from_everyone(): return lax.all_to_all(copies, axis, split_axis=0, concat_axis=0, tiled=True)]
    all_to_all x3 -> x2, starting transfers between devices: 23 us -> 11.7 us  [from_everyone(): return lax.all_to_all(copies, axis, split_axis=0, concat_axis=0, tiled=True)]
    all_to_all x1, blocking collectives: 14.3 us -> 20.1 us  [sum_at_owner(): lax.all_to_all(pieces, axis, split_axis=0, concat_axis=0, tiled=True)]
    all_to_all x0 -> x1, starting transfers between devices: none -> 4.07 us  [map_samples_all(): jax.lax.all_to_all(jnp.stack([arr] * jax.lax.psum(1, axis_name='col'), 0)...]
    another operation x0 -> x1, local copies, waits for them, and re-layouts: none -> 2.98 us  [map_samples_all(): jnp.stack([arr] * jax.lax.psum(1, axis_name='col'), 0)]
    all_to_all x3 -> x2, waiting for transfers between devices: 7.21 us -> 4.24 us  [from_everyone(): return lax.all_to_all(copies, axis, split_axis=0, concat_axis=0, tiled=True)]
  transfers between devices with their start and end apart: 4 -> 3, of which waited for: 4 -> 3; matrix products, arithmetic and copies ran while one was open for 3% -> 3% of each run, Pallas kernels for 0% -> 0%
where the time goes in v1:
time: 227 us
  blocking collectives  70.2 us (31%)
  other arithmetic  59.1 us (26%)
  waiting for transfers between devices  37.7 us (17%)
  matrix products  30.1 us (13%)
  starting transfers between devices  15.8 us (7%)
  local copies, waits for them, and re-layouts  12.8 us (6%)
    all_to_all x3, blocking collectives, from_everyone(): return lax.all_to_all(copies, axis, split_axis=0, concat_axis=0, tiled=True)  50.1 us
    reduce_sum x1, other arithmetic, body(): jnp.sum(dist, axis=1)  35.8 us
    all_to_all x1, waiting for transfers between devices, map_samples_all(): jax.lax.all_to_all(jnp.stack([arr] * jax.lax.psum(1, axis_name='col'), 0)...  33.5 us
    all_to_all x1, blocking collectives, sum_at_owner(): lax.all_to_all(pieces, axis, split_axis=0, concat_axis=0, tiled=True)  20.1 us
    dot_general x1, matrix products, body(): jnp.einsum('ark,bck->abrc', rows, cols, preferred_element_type=jnp.float32)  16 us
    all_to_all x2, starting transfers between devices, from_everyone(): return lax.all_to_all(copies, axis, split_axis=0, concat_axis=0, tiled=True)  11.7 us
    dot_general x1, matrix products, body(): jnp.dot(dist, start_block - block_mean[None, :], precision=highest)  6.79 us
    another operation x3, other arithmetic, body(): lower = jnp.linalg.cholesky(gram)  6.52 us
  transfers between devices with their start and end apart: 3, of which 3 were waited for; matrix products, arithmetic and copies ran while one was open for 3% of the time, Pallas kernels for 0%

profile of v1, /device:TPU:1, one launch (start us, length us, event | category | flops | bytes accessed | tf_op | source)
XLA Modules:
  0.0 226.6 jit_solution(1028833591679327602)
XLA Ops:
  0.6 1.1 reduce_sum.112
  1.7 19.8 %all_to_all.43 = f32[32,1,64]{2,1,0:T(1,128)S(1)} all-to-all(f32[32,1,64]{2,1,0:T(1,128)S(1)} %broadcast_in_dim.11), channel_id=1, replica_groups=mesh['row'=4,'col'=32] {'col'}, dimensions={0} | all-to-all | bytes 16384 | tf_op jit(solution)/shard_map/all_to_all | solution.py:20
  21.5 3.0 %stack.2 = bf16[32,3,32,512]{3,2,1,0:T(8,128)(2,1)} broadcast(bf16[3,32,512]{2,1,0:T(8,128)(2,1)} %param.3), dimensions={1,2,3} | broadcast | bytes 3244032 | tf_op jit(solution)/shard_map/stack | solution.py:13
  24.5 4.1 %all-to-all-start = ((bf16[32,3,32,512]{3,2,1,0:T(8,128)(2,1)}), bf16[32,3,32,512]{3,2,1,0:T(8,128)(2,1)S(1)}, u32[]{:S(2)}, u32[]{:S(2)}) async-start(bf16[32,3,32,512]{3,2,1,0:T(8,128)(2,1)} %stack.2), calls=%async_computation | async-start | bytes 6291456 | tf_op jit(solution)/shard_map/all_to_all | solution.py:13
  28.6 2.5 %convert_reduce_fusion = f32[3,1024]{1,0:T(4,128)S(1)} fusion(bf16[3,1024,512]{2,1,0:T(8,128)(2,1)} %param.4), kind=kLoop, calls=%fused_computation.11 | loop fusion | flops 3142656 | bytes 3158016 | tf_op jit(solution)/shard_map/reduce_sum | solution.py:79
  32.2 1.7 copy-done.2
  34.6 33.5 %all-to-all-done = bf16[32,3,32,512]{3,2,1,0:T(8,128)(2,1)S(1)} async-done(((bf16[32,3,32,512]{3,2,1,0:T(8,128)(2,1)}), bf16[32,3,32,512]{3,2,1,0:T(8,128)(2,1)S(1)}, u32[]{:S(2)}, u32[]{:S(2)}) %all-to-all-start) | async-done | bytes 3145760 | tf_op jit(solution)/shard_map/all_to_all | solution.py:13
  69.6 1.0 fusion.7
  71.5 16.0 %multiply_bitcast_fusion = f32[3,3,1024,1024]{2,3,0,1:T(8,128)} fusion(bf16[3,1024,512]{2,1,0:T(8,128)(2,1)S(1)} %copy-done.3, bf16[3,1024,512]{2,1,0:T(8,128)(2,1)S(1)} %fusion.7), kind=kOutput, calls=%fused_computation | convolution fusion | flops 9673113600 | bytes 44040192 | tf_op jit(solution)/shard_map/ark,bck->abrc/dot_general | solution.py:138
  88.2 35.8 %fusion.70 = (f32[1024]{0:T(1024)S(1)}, f32[1024,1024]{0,1:T(8,128)S(1)}) fusion(f32[3,3,1024,1024]{2,3,0,1:T(8,128)} %multiply_bitcast_fusion, f32[1024]{0:T(1024)S(1)} %get-tuple-element.14, f32[1024]{0:T(1024)S(1)} %get-tuple-element.15), kind=kLoop, calls=%fused_computation.120 | loop fusion | flops 210762752 | bytes 41955328 | tf_op jit(solution)/shard_map/reduce_sum | solution.py:146
  124.0 1.9 copy-done
  125.9 6.8 %fusion.62 = f32[1024,64]{1,0:T(8,128)S(1)} fusion(f32[1024,1024]{0,1:T(8,128)S(1)} %get-tuple-element.13, f32[1024,64]{0,1:T(8,128)S(1)} %copy-done.5, f32[64]{0:T(128)S(1)} %broadcast_multiply_fusion.4), kind=kOutput, calls=%fused_computation.97 | convolution fusion | flops 805371904 | bytes 4718848 | tf_op jit(solution)/shard_map/dot_general | solution.py:145
  133.3 20.1 %all_to_all.44 = f32[32,1,2080]{2,1,0:T(1,128)S(1)} all-to-all(f32[32,1,2080]{2,1,0:T(1,128)S(1)} %all_to_all.30), channel_id=1, replica_groups=mesh['row'=4,'col'=32] {'col'}, dimensions={0} | all-to-all | bytes 532480 | tf_op jit(solution)/shard_map/all_to_all | solution.py:51
  153.7 12.9 %all_to_all.45 = f32[32,1,2080]{2,1,0:T(1,128)S(1)} all-to-all(f32[32,1,2080]{2,1,0:T(1,128)S(1)} %broadcast_in_dim.12), channel_id=1, replica_groups=mesh['row'=4,'col'=32] {'col'}, dimensions={0} | all-to-all | bytes 532480 | tf_op jit(solution)/shard_map/all_to_all | solution.py:20
  168.3 7.8 %all-to-all-start.4 = ((f32[4,1,64]{2,1,0:T(1,128)}), f32[4,1,64]{2,1,0:T(1,128)S(1)}, u32[]{:S(2)}, u32[]{:S(2)}) async-start(f32[4,1,64]{2,1,0:T(1,128)} %broadcast_in_dim.14), calls=%async_computation.4 | async-start | bytes 4096 | tf_op jit(solution)/shard_map/all_to_all | solution.py:20
  176.0 1.0 fusion.57
  178.0 1.0 all-to-all-done.4
  179.0 3.9 %all-to-all-start.5 = ((f32[4,1,4096]{2,1,0:T(1,128)}), f32[4,1,4096]{2,1,0:T(1,128)S(1)}, u32[]{:S(2)}, u32[]{:S(2)}) async-start(f32[4,1,4096]{2,1,0:T(1,128)} %reshape.105), calls=%async_computation.5 | async-start | bytes 131072 | tf_op jit(solution)/shard_map/all_to_all | solution.py:20
  183.0 3.2 %all-to-all-done.5 = f32[4,1,4096]{2,1,0:T(1,128)S(1)} async-done(((f32[4,1,4096]{2,1,0:T(1,128)}), f32[4,1,4096]{2,1,0:T(1,128)S(1)}, u32[]{:S(2)}, u32[]{:S(2)}) %all-to-all-start.5) | async-done | bytes 65568 | tf_op jit(solution)/shard_map/all_to_all | solution.py:20
  187.9 5.8 %cholesky.16 = f32[64,64]{1,0:T(8,128)S(1)} custom-call(f32[64,64]{1,0:T(8,128)S(1)} %fusion.67), custom_call_target="Cholesky" | custom-call | tf_op jit(solution)/shard_map/jit(cholesky)/cholesky | solution.py:157
  195.1 4.9 %custom-call.6 = f32[1,64,64]{1,2,0:T(8,128)S(1)} custom-call(f32[1,64,64]{2,1,0:T(8,128)S(1)} %fusion.65), custom_call_target="InvertDiagBlocksLowerTriangular" | custom-call | tf_op jit(solution)/shard_map/triangular_solve | solution.py:158
  200.8 5.3 %fusion.71 = f32[1024,64]{1,0:T(8,128)S(1)} fusion(f32[1024,1024]{0,1:T(8,128)} %copy-done, f32[1024,64]{0,1:T(8,128)S(1)} %fusion.54), kind=kOutput, calls=%fused_computation.121 | convolution fusion | flops 805306368 | bytes 4718592 | tf_op jit(solution)/shard_map/dot_general | solution.py:161
  207.1 17.3 %all_to_all.46 = f32[4,1,65600]{2,1,0:T(1,128)S(1)} all-to-all(f32[4,1,65600]{2,1,0:T(1,128)S(1)} %broadcast_in_dim.30), channel_id=1, replica_groups=mesh['row'=4,'col'=32] {'row'}, dimensions={0} | all-to-all | bytes 2099200 | tf_op jit(solution)/shard_map/all_to_all | solution.py:20
  224.4 1.0 reduce_sum.119
  (57 shorter events, 14.2 us)
Async XLA Ops:
  24.5 43.6 %all-to-all-start = ((bf16[32,3,32,512]{3,2,1,0:T(8,128)(2,1)}), bf16[32,3,32,512]{3,2,1,0:T(8,128)(2,1)S(1)}, u32[]{:S(2)}, u32[]{:S(2)}) async-start(bf16[32,3,32,512]{3,2,1,0:T(8,128)(2,1)} %stack.2), calls=%async_computation | async-start | bytes 6291456 | tf_op jit(solution)/shard_map/all_to_all | solution.py:13
  28.6 2.8 %copy-start.1 = (bf16[3,1024,512]{2,1,0:T(8,128)(2,1)S(1)}, bf16[3,1024,512]{2,1,0:T(8,128)(2,1)}, u32[]{:S(2)}) copy-start(bf16[3,1024,512]{2,1,0:T(8,128)(2,1)} %param.4) | copy-start | bytes 9437188
  32.2 1.7 copy-start.2
  69.6 1.9 copy-start.3
  88.2 37.7 %copy-start.5 = (f32[1024,64]{0,1:T(8,128)S(1)}, f32[1024,64]{0,1:T(8,128)}, u32[]{:S(2)}) copy-start(f32[1024,64]{0,1:T(8,128)} %param.5) | copy-start | bytes 786436
  124.0 1.9 copy-start
  168.3 10.8 %all-to-all-start.4 = ((f32[4,1,64]{2,1,0:T(1,128)}), f32[4,1,64]{2,1,0:T(1,128)S(1)}, u32[]{:S(2)}, u32[]{:S(2)}) async-start(f32[4,1,64]{2,1,0:T(1,128)} %broadcast_in_dim.14), calls=%async_computation.4 | async-start | bytes 4096 | tf_op jit(solution)/shard_map/all_to_all | solution.py:20
  179.0 7.2 %all-to-all-start.5 = ((f32[4,1,4096]{2,1,0:T(1,128)}), f32[4,1,4096]{2,1,0:T(1,128)S(1)}, u32[]{:S(2)}, u32[]{:S(2)}) async-start(f32[4,1,4096]{2,1,0:T(1,128)} %reshape.105), calls=%async_computation.5 | async-start | bytes 131072 | tf_op jit(solution)/shard_map/all_to_all | solution.py:20
  200.8 23.7 %copy-start.4 = (f32[1024,64]{0,1:T(8,128)}, f32[1024,64]{0,1:T(8,128)S(1)}, u32[]{:S(2)}) copy-start(f32[1024,64]{0,1:T(8,128)S(1)} %fusion.54) | copy-start | bytes 786436
